TPU v7x, 32 devices: a whole 2x2x4 slice. The times are simulated.
32 devices in a mesh: expert: 4 (over z), dp: 8 (over y, x, core).
Axes of the slice: x: 2, y: 2, z: 4, core: 2. Of those that a mesh axis runs over, the one named last changes fastest.
Arguments:
- tokens: bfloat16 [3072, 2304], P(('expert', 'dp')), may hold values from -6 to 6
- expert_ids: int32 [3072, 2], P(('expert', 'dp')), may hold values from 0 to 3, all different within a row; in each aligned block of 96 rows (0 to 95, 96 to 191, ...) at most 64 rows name the same one
- gate_weights: float32 [3072, 2], P(('expert', 'dp')), may hold values from 0.2 to 1
- request_lengths: int32 [32, 4], P(('expert', 'dp')), may hold values from 1 to 48, 96 in all within a row
- request_adapter: int32 [32, 4], P(('expert', 'dp')), may hold values from 0 to 63
- expert_weights: bfloat16 [4, 2, 2304, 5760], P('expert', None, None, 'dp'), may hold values from -0.125 to 0.125
- expert_down: bfloat16 [4, 5760, 2304], P('expert', 'dp'), may hold values from -0.078125 to 0.078125
- low_down: bfloat16 [4, 2304, 2048], P('expert', None, 'dp'), may hold values from -0.125 to 0.125
- low_up: bfloat16 [4, 2, 1024, 5760], P('expert', None, None, 'dp'), may hold values from -1.5 to 1.5
Outputs:
- mixed: bfloat16 [3072, 2304], P(('expert', 'dp'))
Inputs may be any that keep to these rules, and one draw needn't show every extreme that they name: `expert_ids`: each row names 2 different experts; within the rows of one device no expert is named by more than 64 rows, a bound that some block reaches. `request_lengths`: each row sums to 96, and its largest entry is exactly 48.
All inputs are finite; a program needn't handle non-finite values.
Results may differ from a plain program's by a relative error of at most 0.017.
Values may be sent and summed in bfloat16 or wider, within the bound.
No kernel may reach another device: no remote copies, remote signals or barrier semaphores. Data moves between devices by JAX's collectives and lax.ppermute only.
A program may use at most 192 MiB of HBM per device.

v0:
```python
import jax
import jax.numpy as jnp
from jax import lax
from jax.sharding import PartitionSpec as P

TOP = 2
RANK = 16


def body(
    tokens,
    expert_ids,
    gate_weights,
    request_lengths,
    request_adapter,
    expert_weights,
    expert_down,
    low_down,
    low_up,
):
    ways_expert = lax.axis_size("expert")
    local_tokens = tokens.shape[0]
    width = tokens.shape[1]
    experts_all = ways_expert * expert_down.shape[0]
    capacity = local_tokens * TOP * 4 // (3 * experts_all)
    slots_all = experts_all * capacity
    held = low_down.shape[2] // (2 * RANK)
    adapters_all = low_up.shape[2] // RANK
    values = tokens.astype(jnp.float32)
    normed = (values * lax.rsqrt(jnp.mean(values * values, axis=1, keepdims=True) + 1e-05)).astype(
        jnp.bfloat16
    )
    ends = jnp.cumsum(request_lengths[0])
    place = jnp.arange(local_tokens, dtype=jnp.int32)
    which = jnp.sum((place[:, None] >= ends[None, :]).astype(jnp.int32), axis=1)
    lookup = (
        which[:, None] == jnp.arange(request_lengths.shape[1], dtype=jnp.int32)[None, :]
    ).astype(jnp.int32)
    adapter = jnp.sum(lookup * request_adapter[0][None, :], axis=1)
    flat = expert_ids.reshape(-1)
    onehot = (flat[:, None] == jnp.arange(experts_all, dtype=jnp.int32)[None, :]).astype(jnp.int32)
    slot = jnp.sum((jnp.cumsum(onehot, axis=0) - onehot) * onehot, axis=1)
    target = flat * capacity + slot
    placement_weights = (jnp.arange(slots_all, dtype=jnp.int32)[:, None] == target[None, :]).astype(
        jnp.bfloat16
    )
    pairs = jnp.repeat(normed, TOP, axis=0)
    outgoing = (
        jnp.dot(placement_weights, pairs, preferred_element_type=jnp.float32)
        .astype(jnp.bfloat16)
        .reshape(experts_all, capacity, width)
    )
    pair_adapter = jnp.repeat(adapter, TOP).astype(jnp.float32)
    outgoing_ids = (
        jnp.dot(placement_weights.astype(jnp.float32), pair_adapter)
        .astype(jnp.bfloat16)
        .reshape(experts_all, capacity)
    )
    arrived, arrived_ids = (
        lax.all_to_all(outgoing, "expert", split_axis=0, concat_axis=0, tiled=True),
        lax.all_to_all(outgoing_ids, "expert", split_axis=0, concat_axis=0, tiled=True),
    )
    rows, labels_wire = (
        lax.all_gather(arrived.reshape(-1, width), "dp", axis=0, tiled=True),
        lax.all_gather(arrived_ids.reshape(-1), "dp", axis=0, tiled=True),
    )
    rows_total = rows.shape[0]
    labels = labels_wire.astype(jnp.int32)
    group = lax.axis_index("dp")
    projected = jnp.dot(rows, low_down[0], preferred_element_type=jnp.float32).reshape(
        rows_total, held, 2 * RANK
    )
    owned = (labels[:, None] == group * held + jnp.arange(held, dtype=jnp.int32)[None, :]).astype(
        jnp.float32
    )
    lowrank_part = jnp.sum(owned[:, :, None] * projected, axis=1)
    lowrank = lax.psum(lowrank_part.astype(jnp.bfloat16), "dp")
    marks = (labels[:, None] == jnp.arange(adapters_all, dtype=jnp.int32)[None, :]).astype(
        jnp.bfloat16
    )
    spread_gate = (marks[:, :, None] * lowrank[:, None, :RANK]).reshape(
        lax.axis_size("dp") * (ways_expert * capacity), adapters_all * RANK
    )
    sharded_up_weight = (marks[:, :, None] * lowrank[:, None, RANK:]).reshape(
        lax.axis_size("dp") * (ways_expert * capacity), adapters_all * RANK
    )
    gate = jnp.dot(rows, expert_weights[0, 0], preferred_element_type=jnp.float32) + jnp.dot(
        spread_gate, low_up[0, 0], preferred_element_type=jnp.float32
    )
    up = jnp.dot(rows, expert_weights[0, 1], preferred_element_type=jnp.float32) + jnp.dot(
        sharded_up_weight, low_up[0, 1], preferred_element_type=jnp.float32
    )
    hidden_activations = (jax.nn.silu(gate) * up).astype(jnp.bfloat16)
    mine = lax.psum_scatter(
        jnp.dot(hidden_activations, expert_down[0], preferred_element_type=jnp.float32).astype(
            jnp.bfloat16
        ),
        "dp",
        scatter_dimension=0,
        tiled=True,
    ).astype(jnp.float32)
    mine = mine.astype(jnp.bfloat16).reshape(ways_expert, capacity, width)
    back = lax.all_to_all(mine, "expert", split_axis=0, concat_axis=0, tiled=True)
    picked = jnp.dot(
        placement_weights.T, back.reshape(slots_all, width), preferred_element_type=jnp.float32
    ).reshape(local_tokens, TOP, width)
    mixed = values + jnp.sum(gate_weights[:, :, None] * picked, axis=1)
    return mixed.astype(jnp.bfloat16)


def solution(mesh):
    return jax.shard_map(
        body,
        mesh=mesh,
        in_specs=(
            P(("expert", "dp"), None),
            P(("expert", "dp"), None),
            P(("expert", "dp"), None),
            P(("expert", "dp"), None),
            P(("expert", "dp"), None),
            P("expert", None, None, "dp"),
            P("expert", "dp", None),
            P("expert", None, "dp"),
            P("expert", None, None, "dp"),
        ),
        out_specs=P(("expert", "dp"), None),
        check_vma=False,
    )
```

profile of v0, /device:TPU:0, one launch (start us, length us, event | category | flops | bytes accessed | tf_op | source)
XLA Modules:
  0.0 319.4 jit_solution(102362111478720045)
XLA Ops:
  6.5 0.0 copy-start
  6.5 0.0 all-gather.3.cloned.1.call-start
  6.5 0.9 copy.24
  7.5 0.1 reshape.192
  7.6 1.2 reduce-window.18
  8.9 0.1 slice.36
  8.9 0.1 copy.25
  9.1 0.1 copy.26
  9.2 0.1 add_bitcast_fusion
  9.3 1.2 fusion.24
  10.5 1.2 fusion.25
  11.7 0.0 copy-start.3
  11.7 0.0 copy-start.4
  11.7 1.4 broadcast_in_dim.4
  13.1 3.1 reshape.195
  16.2 1.6 convolution_convert_fusion.1
  17.9 34.8 %all_to_all.20 = bf16[4,64,2304]{2,1,0:T(8,128)(2,1)} all-to-all(bf16[4,64,2304]{2,1,0:T(8,128)(2,1)S(1)} %bitcast.58), channel_id=1, replica_groups=mesh['expert'=4,'dp'=8] {'expert'}, dimensions={0} | all-to-all | bytes 2359296 | tf_op jit(solution)/shard_map/all_to_all | solution.py:60
  52.6 0.0 all-gather.3.cloned.1.call-update
  52.7 0.0 copy-done.3
  52.7 0.2 reduce-window.20
  52.8 0.1 convert_reduce_fusion
  52.9 0.0 copy-done.4
  52.9 0.1 select_reduce_fusion
  53.0 0.1 broadcast_in_dim.5
  53.1 0.2 reshape.208
  53.3 0.2 fusion.28
  53.4 0.7 all_to_all.16
  54.1 3.2 %all-to-all-start.1 = ((bf16[4,1,64]{2,1,0:T(2,128)(2,1)}), bf16[4,1,64]{2,1,0:T(2,128)(2,1)S(1)}, u32[]{:S(2)}, u32[]{:S(2)}) async-start(bf16[4,1,64]{2,1,0:T(2,128)(2,1)} %all_to_all.16), calls=%async_computation.1 | async-start | bytes 4096 | tf_op jit(solution)/shard_map/all_to_all | solution.py:61
  57.4 0.0 all-reduce.3.cloned.1.call-start
  57.4 2.4 copy.28
  59.9 2.9 all-to-all-done.1
  62.8 0.1 reshape.204
  62.9 8.9 %all-gather = bf16[8,1,256]{2,1,0:T(2,128)(2,1)S(1)} all-gather(bf16[1,1,256]{2,1,0:T(2,128)(2,1)S(1)} %reshape.204), channel_id=1, replica_groups=mesh['expert'=4,'dp'=8] {'dp'}, dimensions={0}, use_global_device_ids=true | all-gather | bytes 4608 | tf_op jit(solution)/shard_map/all_gather | solution.py:65
  71.8 0.1 compare_convert_fusion
  71.9 0.8 fusion.27
  72.6 38.1 %all-gather.3.cloned.1.call-done = bf16[2048,2304]{1,0:T(8,128)(2,1)} async-done(((bf16[256,2304]{1,0:T(8,128)(2,1)}), bf16[2048,2304]{1,0:T(8,128)(2,1)}) %all-gather.3.cloned.1.call-update) | async-done | bytes 9437200 | tf_op jit(solution)/shard_map/all_gather | solution.py:64
  110.8 7.3 %fusion.21 = bf16[2048,32]{0,1:T(8,128)(2,1)} fusion(bf16[8,32,2304]{2,1,0:T(8,128)(2,1)} %bitcast.62, bf16[2048,2304]{1,0:T(8,128)(2,1)} %all-gather.3.cloned.1.call-done, f32[2048,8]{0,1:T(8,128)S(1)} %compare_convert_fusion), kind=kOutput, calls=%fused_computation.23 | convolution fusion | flops 2416902144 | bytes 10813440 | tf_op jit(solution)/shard_map/dot_general | solution.py:70
  118.0 0.0 all-reduce.3.cloned.1.call-update
  118.1 0.2 reduce-scatter.2.cloned.1.call-start
  118.3 12.2 %fusion.3 = f32[2048,720]{0,1:T(8,128)} fusion(bf16[2048,2304]{1,0:T(8,128)(2,1)} %all-gather.3.cloned.1.call-done, bf16[1,2,2304,720]{2,3,1,0:T(8,128)(2,1)} %param.14), kind=kOutput, calls=%fused_computation.7 | convolution fusion | flops 6794772480 | bytes 18653184 | tf_op jit(solution)/shard_map/dot_general | solution.py:90
  130.5 12.2 %fusion.5 = f32[2048,720]{0,1:T(8,128)} fusion(bf16[2048,2304]{1,0:T(8,128)(2,1)} %all-gather.3.cloned.1.call-done, bf16[1,2,2304,720]{2,3,1,0:T(8,128)(2,1)} %param.14), kind=kOutput, calls=%fused_computation.9 | convolution fusion | flops 6794772480 | bytes 18653184 | tf_op jit(solution)/shard_map/dot_general | solution.py:87
  142.8 28.4 %all-reduce.3.cloned.1.call-done = bf16[2048,32]{0,1:T(8,128)(2,1)} async-done(((bf16[2048,32]{0,1:T(8,128)(2,1)}), bf16[2048,32]{0,1:T(8,128)(2,1)}) %all-reduce.3.cloned.1.call-update) | async-done | bytes 131088 | tf_op jit(solution)/shard_map/psum | solution.py:77
  171.2 0.9 fusion.35
  172.1 0.0 copy-start.2
  172.1 3.7 %broadcast_multiply_fusion = (bf16[2048,64,16]{0,2,1:T(8,128)(2,1)}, bf16[2048,64,16]{0,2,1:T(8,128)(2,1)S(1)}) fusion(bf16[2048,16]{0,1:T(8,128)(2,1)S(1)} %get-tuple-element.7, bf16[2048,64]{0,1:T(8,128)(2,1)} %fusion.27, bf16[2048,16]{0,1:T(8,128)(2,1)S(1)} %get-tuple-element.8), kind=kLoop, calls=%fused_computation.15 | loop fusion | flops 4194304 | bytes 8781824 | tf_op jit(solution)/shard_map/mul | solution.py:84
  175.8 0.0 copy-done.2
  175.8 5.2 %fusion.15 = f32[2048,720]{0,1:T(8,128)} fusion(bf16[2048,1024]{0,1:T(8,128)(2,1)S(1)} %bitcast.61, bf16[1,2,1024,720]{2,3,1,0:T(8,128)(2,1)S(1)} %copy-done.2), kind=kOutput, calls=%fused_computation.18 | convolution fusion | flops 3019898880 | bytes 11567104 | tf_op jit(solution)/shard_map/dot_general | solution.py:87
  181.0 0.0 copy-done
  181.0 18.9 %convolution_convert_fusion = bf16[2048,2304]{1,0:T(8,128)(2,1)} fusion(bf16[1,720,2304]{2,1,0:T(8,128)(2,1)S(1)} %copy-done, f32[2048,720]{0,1:T(8,128)} %fusion.3, f32[2048,720]{0,1:T(8,128)} %fusion.5, f32[2048,720]{0,1:T(8,128)} %fusion.15, bf16[2048,1024]{0,1:T(8,128)(2,1)} %bitcast.60, bf16[1,2,1024,720]{2,3,1,0:T(8,128)(2,1)} %param.17), kind=kOutput, calls=%fused_computation | convolution fusion | flops 9831186432 | bytes 36118528 | tf_op jit(solution)/shard_map/dot_general | solution.py:95
  199.9 0.0 copy-start.1
  199.9 0.0 reduce-scatter.2.cloned.1.call-update
  199.9 76.0 %reduce-scatter.2.cloned.1.call-done = bf16[256,2304]{1,0:T(8,128)(2,1)} async-done(((bf16[2048,2304]{1,0:T(8,128)(2,1)}), bf16[256,2304]{1,0:T(8,128)(2,1)}) %reduce-scatter.2.cloned.1.call-update) | async-done | bytes 1179664 | tf_op jit(solution)/shard_map/reduce_scatter | solution.py:94
  276.0 4.6 %all-to-all-start.2 = ((bf16[4,64,2304]{2,1,0:T(8,128)(2,1)}), bf16[4,64,2304]{2,1,0:T(8,128)(2,1)}, u32[]{:S(2)}, u32[]{:S(2)}) async-start(bf16[4,64,2304]{2,1,0:T(8,128)(2,1)} %bitcast.63), calls=%async_computation.3 | async-start | bytes 2359296 | tf_op jit(solution)/shard_map/all_to_all | solution.py:103
  280.6 0.1 iota_compare_fusion.4
  280.7 0.1 eq.104
  280.7 28.5 %all-to-all-done.2 = bf16[4,64,2304]{2,1,0:T(8,128)(2,1)} async-done(((bf16[4,64,2304]{2,1,0:T(8,128)(2,1)}), bf16[4,64,2304]{2,1,0:T(8,128)(2,1)}, u32[]{:S(2)}, u32[]{:S(2)}) %all-to-all-start.2) | async-done | bytes 1179680 | tf_op jit(solution)/shard_map/all_to_all | solution.py:103
  309.2 0.0 copy-done.1
  309.2 1.7 fusion.20
  311.0 1.9 fusion.26
  (14 shorter events, 0.2 us)
Async XLA Ops:
  6.5 174.4 %copy-start = (bf16[1,720,2304]{2,1,0:T(8,128)(2,1)S(1)}, bf16[1,720,2304]{2,1,0:T(8,128)(2,1)}, u32[]{:S(2)}) copy-start(bf16[1,720,2304]{2,1,0:T(8,128)(2,1)} %param.15) | copy-start | bytes 9953284
  6.5 104.2 %all-gather.3.cloned.1.call-start = ((), (), s32[]{:S(2)}) async-start(), calls=%async_computation.4 | async-start | bytes 10616832 | tf_op jit(solution)/shard_map/all_gather | solution.py:64
  11.7 41.0 %copy-start.3 = (s32[1,4]{1,0:T(1,128)S(1)}, s32[1,4]{1,0:T(1,128)}, u32[]{:S(2)}) copy-start(s32[1,4]{1,0:T(1,128)} %param.12) | copy-start | bytes 52
  11.7 41.2 %copy-start.4 = (s32[1,4]{1,0:T(1,128)S(1)}, s32[1,4]{1,0:T(1,128)}, u32[]{:S(2)}) copy-start(s32[1,4]{1,0:T(1,128)} %param.13) | copy-start | bytes 52
  54.1 8.7 %all-to-all-start.1 = ((bf16[4,1,64]{2,1,0:T(2,128)(2,1)}), bf16[4,1,64]{2,1,0:T(2,128)(2,1)S(1)}, u32[]{:S(2)}, u32[]{:S(2)}) async-start(bf16[4,1,64]{2,1,0:T(2,128)(2,1)} %all_to_all.16), calls=%async_computation.1 | async-start | bytes 4096 | tf_op jit(solution)/shard_map/all_to_all | solution.py:61
  57.4 113.8 %all-reduce.3.cloned.1.call-start = ((), (), s32[]{:S(2)}) async-start(), calls=%async_computation.5 | async-start | bytes 262144 | tf_op jit(solution)/shard_map/psum | solution.py:77
  118.1 157.9 %reduce-scatter.2.cloned.1.call-start = ((), (), s32[]{:S(2)}) async-start(), calls=%async_computation.6 | async-start | bytes 10616832 | tf_op jit(solution)/shard_map/reduce_scatter | solution.py:94
  172.1 3.7 %copy-start.2 = (bf16[1,2,1024,720]{2,3,1,0:T(8,128)(2,1)S(1)}, bf16[1,2,1024,720]{2,3,1,0:T(8,128)(2,1)}, u32[]{:S(2)}) copy-start(bf16[1,2,1024,720]{2,3,1,0:T(8,128)(2,1)} %param.17) | copy-start | bytes 8847364
  199.9 109.3 %copy-start.1 = (f32[96,2]{0,1:T(2,128)S(1)}, f32[96,2]{0,1:T(2,128)}, u32[]{:S(2)}) copy-start(f32[96,2]{0,1:T(2,128)} %param.11) | copy-start | bytes 2308
  276.0 33.2 %all-to-all-start.2 = ((bf16[4,64,2304]{2,1,0:T(8,128)(2,1)}), bf16[4,64,2304]{2,1,0:T(8,128)(2,1)}, u32[]{:S(2)}, u32[]{:S(2)}) async-start(bf16[4,64,2304]{2,1,0:T(8,128)(2,1)} %bitcast.63), calls=%async_computation.3 | async-start | bytes 2359296 | tf_op jit(solution)/shard_map/all_to_all | solution.py:103
Sparse Core Ops, SparseCore 0:
  52.8 57.9 all-gather.2
  118.2 52.9 all-reduce.2
  200.1 75.8 reduce-scatter.1
where the time goes:
time: 320 us; the launch traced here: 319 us
  waiting for transfers between devices  174 us (54%)
  matrix products  59.4 us (19%)
  blocking collectives  43.7 us (14%)
  between operations  13.3 us (4%)
  other arithmetic  10.7 us (3%)
  local copies, waits for them, and re-layouts  10.3 us (3%)
  starting transfers between devices  8.09 us (3%)
    reduce_scatter x1, waiting for transfers between devices, body(): lax.psum_scatter(jnp.dot(hidden_activations, expert_down[0], preferred_el...  76 us
    all_gather x1, waiting for transfers between devices, body(): lax.all_gather(arrived.reshape(-1, width), 'dp', axis=0, tiled=True)  38.1 us
    all_to_all x1, blocking collectives, body(): lax.all_to_all(outgoing, 'expert', split_axis=0, concat_axis=0, tiled=True)  34.8 us
    all_to_all x1, waiting for transfers between devices, body(): lax.all_to_all(mine, 'expert', split_axis=0, concat_axis=0, tiled=True)  28.5 us
    psum x1, waiting for transfers between devices, body(): lowrank = lax.psum(lowrank_part.astype(jnp.bfloat16), 'dp')  28.4 us
    dot_general x1, matrix products, body(): jnp.dot(hidden_activations, expert_down[0], preferred_element_type=jnp.fl...  18.9 us
    dot_general x1, matrix products, body(): jnp.dot(rows, expert_weights[0, 0], preferred_element_type=jnp.float32)  12.2 us
    dot_general x1, matrix products, body(): jnp.dot(rows, expert_weights[0, 1], preferred_element_type=jnp.float32)  12.2 us
  transfers between devices with their start and end apart: 5, of which 5 were waited for; matrix products, arithmetic and copies ran while one was open for 9% of the time, Pallas kernels for 0%

commit v1 on v0

--- a/solution.py
+++ b/solution.py
@@ -5,6 +5,22 @@
 
 TOP = 2
 RANK = 16
+
+
+def collect(x, axis, dim):
+    ways, here, step = (lax.axis_size(axis), lax.axis_index(axis), x.shape[dim])
+    shape = [n * ways if d == dim else n for d, n in enumerate(x.shape)]
+    full = lax.dynamic_update_slice_in_dim(jnp.zeros(shape, x.dtype), x, here * step, axis=dim)
+    going_up = going_down = x
+    for far in range(1, ways // 2 + 1):
+        going_up = lax.ppermute(going_up, axis, [(d, (d + 1) % ways) for d in range(ways)])
+        full = lax.dynamic_update_slice_in_dim(full, going_up, (here - far) % ways * step, axis=dim)
+        if 2 * far < ways:
+            going_down = lax.ppermute(going_down, axis, [(d, (d - 1) % ways) for d in range(ways)])
+            full = lax.dynamic_update_slice_in_dim(
+                full, going_down, (here + far) % ways * step, axis=dim
+            )
+    return full
 
 
 def body(
@@ -62,7 +78,7 @@
     )
     rows, labels_wire = (
         lax.all_gather(arrived.reshape(-1, width), "dp", axis=0, tiled=True),
-        lax.all_gather(arrived_ids.reshape(-1), "dp", axis=0, tiled=True),
+        collect(arrived_ids.reshape(-1), "dp", 0),
     )
     rows_total = rows.shape[0]
     labels = labels_wire.astype(jnp.int32)

time: 320 us -> 320 us (level)
  blocking collectives: 43.7 us -> 34.8 us
  starting transfers between devices: 8.09 us -> 16 us
    all_gather x1 -> x0, blocking collectives: 8.9 us -> none  [body(): lax.all_gather(arrived_ids.reshape(-1), 'dp', axis=0, tiled=True)]
    all_gather x1, waiting for transfers between devices: 38.1 us -> 30.1 us  [body(): lax.all_gather(arrived.reshape(-1, width), 'dp', axis=0, tiled=True)]
    ppermute x0 -> x7, starting transfers between devices: none -> 7.94 us  [the longest x3 7.93 us: collect(): lax.ppermute(going_down, axis, [(d, (d - 1) % ways) for d in range(ways)])]
    ppermute x0 -> x7, waiting for transfers between devices: none -> 4.93 us  [the longest x4 3.61 us: collect(): lax.ppermute(going_up, axis, [(d, (d + 1) % ways) for d in range(ways)])]
  transfers between devices with their start and end apart: 5 -> 12, of which waited for: 5 -> 8; matrix products, arithmetic and copies ran while one was open for 9% -> 9% of each run, Pallas kernels for 0% -> 0%
where the time goes in v1:
time: 320 us; the launch traced here: 319 us
  waiting for transfers between devices  173 us (54%)
  matrix products  59.4 us (19%)
  blocking collectives  34.8 us (11%)
  starting transfers between devices  16 us (5%)
  between operations  13.4 us (4%)
  local copies, waits for them, and re-layouts  11.8 us (4%)
  other arithmetic  10.7 us (3%)
    reduce_scatter x1, waiting for transfers between devices, body(): lax.psum_scatter(jnp.dot(hidden_activations, expert_down[0], preferred_el...  76 us
    all_to_all x1, blocking collectives, body(): lax.all_to_all(outgoing, 'expert', split_axis=0, concat_axis=0, tiled=True)  34.8 us
    all_gather x1, waiting for transfers between devices, body(): lax.all_gather(arrived.reshape(-1, width), 'dp', axis=0, tiled=True)  30.1 us
    all_to_all x1, waiting for transfers between devices, body(): lax.all_to_all(mine, 'expert', split_axis=0, concat_axis=0, tiled=True)  28.5 us
    psum x1, waiting for transfers between devices, body(): lowrank = lax.psum(lowrank_part.astype(jnp.bfloat16), 'dp')  28.4 us
    dot_general x1, matrix products, body(): jnp.dot(hidden_activations, expert_down[0], preferred_element_type=jnp.fl...  18.9 us
    dot_general x1, matrix products, body(): jnp.dot(rows, expert_weights[0, 0], preferred_element_type=jnp.float32)  12.2 us
    dot_general x1, matrix products, body(): jnp.dot(rows, expert_weights[0, 1], preferred_element_type=jnp.float32)  12.2 us
  transfers between devices with their start and end apart: 12, of which 8 were waited for; matrix products, arithmetic and copies ran while one was open for 9% of the time, Pallas kernels for 0%

profile of v1, /device:TPU:0, one launch (start us, length us, event | category | flops | bytes accessed | tf_op | source)
XLA Modules:
  0.0 319.3 jit_solution(6643834911162599803)
XLA Ops:
  6.5 0.9 copy.24
  7.5 0.1 reshape.192
  7.6 1.2 reduce-window.18
  8.9 0.1 slice.36
  8.9 0.1 copy.25
  9.1 0.1 copy.26
  9.2 0.1 add_bitcast_fusion
  9.3 1.2 fusion.24
  10.5 1.2 fusion.25
  11.7 0.0 copy-start.3
  11.7 0.0 copy-start.4
  11.7 1.4 broadcast_in_dim.6
  13.1 3.1 reshape.195
  16.2 1.6 convolution_convert_fusion.1
  17.9 34.8 %all_to_all.20 = bf16[4,64,2304]{2,1,0:T(8,128)(2,1)} all-to-all(bf16[4,64,2304]{2,1,0:T(8,128)(2,1)S(1)} %bitcast.57), channel_id=1, replica_groups=mesh['expert'=4,'dp'=8] {'expert'}, dimensions={0} | all-to-all | bytes 2359296 | tf_op jit(solution)/shard_map/all_to_all | solution.py:76
  52.6 0.0 all-gather.2.cloned.1.call-update
  52.7 0.2 reduce-window.20
  52.8 0.1 convert_reduce_fusion
  52.9 0.1 select_reduce_fusion
  53.0 0.1 broadcast_in_dim.8
  53.1 0.2 reshape.204
  53.3 0.2 fusion.28
  53.4 0.7 all_to_all.16
  54.1 3.2 %all-to-all-start.1 = ((bf16[4,1,64]{2,1,0:T(2,128)(2,1)}), bf16[4,1,64]{2,1,0:T(2,128)(2,1)S(1)}, u32[]{:S(2)}, u32[]{:S(2)}) async-start(bf16[4,1,64]{2,1,0:T(2,128)(2,1)} %all_to_all.16), calls=%async_computation.1 | async-start | bytes 4096 | tf_op jit(solution)/shard_map/all_to_all | solution.py:77
  57.4 0.0 all-reduce.3.cloned.1.call-start
  57.5 5.3 %all-to-all-done.1 = bf16[4,1,64]{2,1,0:T(2,128)(2,1)S(1)} async-done(((bf16[4,1,64]{2,1,0:T(2,128)(2,1)}), bf16[4,1,64]{2,1,0:T(2,128)(2,1)S(1)}, u32[]{:S(2)}, u32[]{:S(2)}) %all-to-all-start.1) | async-done | bytes 544 | tf_op jit(solution)/shard_map/all_to_all | solution.py:77
  62.8 0.1 reshape.200
  62.9 2.6 collective-permute-start.1
  65.6 1.2 collective-permute-done
  66.8 2.4 copy.28
  69.2 2.6 collective-permute-start.3
  71.8 1.3 collective-permute-done.3
  73.1 2.6 collective-permute-start.5
  75.7 0.3 dynamic_update_slice.24
  76.0 0.2 dynamic_update_slice.25
  76.2 0.2 dynamic_update_slice.26
  76.4 0.2 dynamic_update_slice.27
  76.6 0.2 dynamic_update_slice.28
  76.8 0.2 dynamic_update_slice.29
  77.0 0.0 collective-permute-done.5
  77.0 0.2 dynamic_update_slice.30
  77.2 2.4 collective-permute-done.6
  79.6 0.2 dynamic_update_slice.31
  79.8 0.1 compare_convert_fusion
  79.9 0.8 fusion.27
  80.6 30.1 %all-gather.2.cloned.1.call-done = bf16[2048,2304]{1,0:T(8,128)(2,1)} async-done(((bf16[256,2304]{1,0:T(8,128)(2,1)}), bf16[2048,2304]{1,0:T(8,128)(2,1)}) %all-gather.2.cloned.1.call-update) | async-done | bytes 9437200 | tf_op jit(solution)/shard_map/all_gather | solution.py:80
  110.8 7.3 %fusion.21 = bf16[2048,32]{0,1:T(8,128)(2,1)} fusion(bf16[8,32,2304]{2,1,0:T(8,128)(2,1)} %bitcast.61, bf16[2048,2304]{1,0:T(8,128)(2,1)} %all-gather.2.cloned.1.call-done, f32[2048,8]{0,1:T(8,128)S(1)} %compare_convert_fusion), kind=kOutput, calls=%fused_computation.23 | convolution fusion | flops 2416902144 | bytes 10813440 | tf_op jit(solution)/shard_map/dot_general | solution.py:86
  118.0 0.0 all-reduce.3.cloned.1.call-update
  118.1 0.2 reduce-scatter.2.cloned.1.call-start
  118.3 12.2 %fusion.3 = f32[2048,720]{0,1:T(8,128)} fusion(bf16[2048,2304]{1,0:T(8,128)(2,1)} %all-gather.2.cloned.1.call-done, bf16[1,2,2304,720]{2,3,1,0:T(8,128)(2,1)} %param.14), kind=kOutput, calls=%fused_computation.7 | convolution fusion | flops 6794772480 | bytes 18653184 | tf_op jit(solution)/shard_map/dot_general | solution.py:106
  130.5 12.2 %fusion.5 = f32[2048,720]{0,1:T(8,128)} fusion(bf16[2048,2304]{1,0:T(8,128)(2,1)} %all-gather.2.cloned.1.call-done, bf16[1,2,2304,720]{2,3,1,0:T(8,128)(2,1)} %param.14), kind=kOutput, calls=%fused_computation.9 | convolution fusion | flops 6794772480 | bytes 18653184 | tf_op jit(solution)/shard_map/dot_general | solution.py:103
  142.7 28.4 %all-reduce.3.cloned.1.call-done = bf16[2048,32]{0,1:T(8,128)(2,1)} async-done(((bf16[2048,32]{0,1:T(8,128)(2,1)}), bf16[2048,32]{0,1:T(8,128)(2,1)}) %all-reduce.3.cloned.1.call-update) | async-done | bytes 131088 | tf_op jit(solution)/shard_map/psum | solution.py:93
  171.2 0.9 fusion.35
  172.1 3.7 %broadcast_multiply_fusion = (bf16[2048,64,16]{0,2,1:T(8,128)(2,1)}, bf16[2048,64,16]{0,2,1:T(8,128)(2,1)S(1)}) fusion(bf16[2048,16]{0,1:T(8,128)(2,1)S(1)} %get-tuple-element.7, bf16[2048,64]{0,1:T(8,128)(2,1)} %fusion.27, bf16[2048,16]{0,1:T(8,128)(2,1)S(1)} %get-tuple-element.8), kind=kLoop, calls=%fused_computation.15 | loop fusion | flops 4194304 | bytes 8781824 | tf_op jit(solution)/shard_map/mul | solution.py:100
  175.8 5.2 %fusion.15 = f32[2048,720]{0,1:T(8,128)} fusion(bf16[2048,1024]{0,1:T(8,128)(2,1)S(1)} %bitcast.60, bf16[1,2,1024,720]{2,3,1,0:T(8,128)(2,1)S(1)} %copy-done.2), kind=kOutput, calls=%fused_computation.18 | convolution fusion | flops 3019898880 | bytes 11567104 | tf_op jit(solution)/shard_map/dot_general | solution.py:103
  181.0 18.9 %convolution_convert_fusion = bf16[2048,2304]{1,0:T(8,128)(2,1)} fusion(bf16[1,720,2304]{2,1,0:T(8,128)(2,1)S(1)} %copy-done, f32[2048,720]{0,1:T(8,128)} %fusion.3, f32[2048,720]{0,1:T(8,128)} %fusion.5, f32[2048,720]{0,1:T(8,128)} %fusion.15, bf16[2048,1024]{0,1:T(8,128)(2,1)} %bitcast.59, bf16[1,2,1024,720]{2,3,1,0:T(8,128)(2,1)} %param.17), kind=kOutput, calls=%fused_computation | convolution fusion | flops 9831186432 | bytes 36118528 | tf_op jit(solution)/shard_map/dot_general | solution.py:111
  199.9 0.0 reduce-scatter.2.cloned.1.call-update
  199.9 76.0 %reduce-scatter.2.cloned.1.call-done = bf16[256,2304]{1,0:T(8,128)(2,1)} async-done(((bf16[2048,2304]{1,0:T(8,128)(2,1)}), bf16[256,2304]{1,0:T(8,128)(2,1)}) %reduce-scatter.2.cloned.1.call-update) | async-done | bytes 1179664 | tf_op jit(solution)/shard_map/reduce_scatter | solution.py:110
  275.9 4.6 %all-to-all-start.2 = ((bf16[4,64,2304]{2,1,0:T(8,128)(2,1)}), bf16[4,64,2304]{2,1,0:T(8,128)(2,1)}, u32[]{:S(2)}, u32[]{:S(2)}) async-start(bf16[4,64,2304]{2,1,0:T(8,128)(2,1)} %bitcast.62), calls=%async_computation.3 | async-start | bytes 2359296 | tf_op jit(solution)/shard_map/all_to_all | solution.py:119
  280.6 0.1 iota_compare_fusion.4
  280.7 0.1 eq.112
  280.7 28.5 %all-to-all-done.2 = bf16[4,64,2304]{2,1,0:T(8,128)(2,1)} async-done(((bf16[4,64,2304]{2,1,0:T(8,128)(2,1)}), bf16[4,64,2304]{2,1,0:T(8,128)(2,1)}, u32[]{:S(2)}, u32[]{:S(2)}) %all-to-all-start.2) | async-done | bytes 1179680 | tf_op jit(solution)/shard_map/all_to_all | solution.py:119
  309.2 1.7 fusion.20
  310.9 1.9 fusion.26
  (31 shorter events, 0.2 us)
Async XLA Ops:
  6.5 174.4 %copy-start = (bf16[1,720,2304]{2,1,0:T(8,128)(2,1)S(1)}, bf16[1,720,2304]{2,1,0:T(8,128)(2,1)}, u32[]{:S(2)}) copy-start(bf16[1,720,2304]{2,1,0:T(8,128)(2,1)} %param.15) | copy-start | bytes 9953284
  6.5 104.2 %all-gather.2.cloned.1.call-start = ((), (), s32[]{:S(2)}) async-start(), calls=%async_computation.4 | async-start | bytes 10616832 | tf_op jit(solution)/shard_map/all_gather | solution.py:80
  11.7 41.0 %copy-start.3 = (s32[1,4]{1,0:T(1,128)S(1)}, s32[1,4]{1,0:T(1,128)}, u32[]{:S(2)}) copy-start(s32[1,4]{1,0:T(1,128)} %param.12) | copy-start | bytes 52
  11.7 41.2 %copy-start.4 = (s32[1,4]{1,0:T(1,128)S(1)}, s32[1,4]{1,0:T(1,128)}, u32[]{:S(2)}) copy-start(s32[1,4]{1,0:T(1,128)} %param.13) | copy-start | bytes 52
  54.1 8.7 %all-to-all-start.1 = ((bf16[4,1,64]{2,1,0:T(2,128)(2,1)}), bf16[4,1,64]{2,1,0:T(2,128)(2,1)S(1)}, u32[]{:S(2)}, u32[]{:S(2)}) async-start(bf16[4,1,64]{2,1,0:T(2,128)(2,1)} %all_to_all.16), calls=%async_computation.1 | async-start | bytes 4096 | tf_op jit(solution)/shard_map/all_to_all | solution.py:77
  57.4 113.8 %all-reduce.3.cloned.1.call-start = ((), (), s32[]{:S(2)}) async-start(), calls=%async_computation.5 | async-start | bytes 262144 | tf_op jit(solution)/shard_map/psum | solution.py:93
  62.9 3.9 %collective-permute-start = (bf16[256]{0:T(256)(128)(2,1)S(1)}, bf16[256]{0:T(256)(128)(2,1)S(1)}, u32[]{:S(2)}, u32[]{:S(2)}) collective-permute-start(bf16[256]{0:T(256)(128)(2,1)S(1)} %reshape.200), channel_id=1, source_target_pairs={{0,1},{1,2},{2,3},{3,4},{4,5},{5,6},{6,7},{7,0},{8,9},{9,10},{10,1... | collective-permute-start | bytes 1544 | tf_op jit(solution)/shard_map/ppermute | solution.py:16
  62.9 6.2 %collective-permute-start.1 = (bf16[256]{0:T(256)(128)(2,1)S(1)}, bf16[256]{0:T(256)(128)(2,1)S(1)}, u32[]{:S(2)}, u32[]{:S(2)}) collective-permute-start(bf16[256]{0:T(256)(128)(2,1)S(1)} %reshape.200), channel_id=1, source_target_pairs={{0,7},{1,0},{2,1},{3,2},{4,3},{5,4},{6,5},{7,6},{8,15},{9,8},{10,9... | collective-permute-start | bytes 1544 | tf_op jit(solution)/shard_map/ppermute | solution.py:19
  66.8 5.0 %collective-permute-start.2 = (bf16[256]{0:T(256)(128)(2,1)S(1)}, bf16[256]{0:T(256)(128)(2,1)S(1)}, u32[]{:S(2)}, u32[]{:S(2)}) collective-permute-start(bf16[256]{0:T(256)(128)(2,1)S(1)} %collective-permute-done), channel_id=1, source_target_pairs={{0,1},{1,2},{2,3},{3,4},{4,5},{5,6},{6,7},{7,0},{8,9},{9,10},{10,1... | collective-permute-start | bytes 1544 | tf_op jit(solution)/shard_map/ppermute | solution.py:16
  69.2 3.9 %collective-permute-start.3 = (bf16[256]{0:T(256)(128)(2,1)S(1)}, bf16[256]{0:T(256)(128)(2,1)S(1)}, u32[]{:S(2)}, u32[]{:S(2)}) collective-permute-start(bf16[256]{0:T(256)(128)(2,1)S(1)} %collective-permute-done.1), channel_id=1, source_target_pairs={{0,7},{1,0},{2,1},{3,2},{4,3},{5,4},{6,5},{7,6},{8,15},{9,8},{10,9... | collective-permute-start | bytes 1544 | tf_op jit(solution)/shard_map/ppermute | solution.py:19
  71.8 3.9 %collective-permute-start.4 = (bf16[256]{0:T(256)(128)(2,1)S(1)}, bf16[256]{0:T(256)(128)(2,1)S(1)}, u32[]{:S(2)}, u32[]{:S(2)}) collective-permute-start(bf16[256]{0:T(256)(128)(2,1)S(1)} %collective-permute-done.2), channel_id=1, source_target_pairs={{0,1},{1,2},{2,3},{3,4},{4,5},{5,6},{6,7},{7,0},{8,9},{9,10},{10,1... | collective-permute-start | bytes 1544 | tf_op jit(solution)/shard_map/ppermute | solution.py:16
  73.1 3.9 %collective-permute-start.5 = (bf16[256]{0:T(256)(128)(2,1)S(1)}, bf16[256]{0:T(256)(128)(2,1)S(1)}, u32[]{:S(2)}, u32[]{:S(2)}) collective-permute-start(bf16[256]{0:T(256)(128)(2,1)S(1)} %collective-permute-done.3), channel_id=1, source_target_pairs={{0,7},{1,0},{2,1},{3,2},{4,3},{5,4},{6,5},{7,6},{8,15},{9,8},{10,9... | collective-permute-start | bytes 1544 | tf_op jit(solution)/shard_map/ppermute | solution.py:19
  75.7 3.9 %collective-permute-start.6 = (bf16[256]{0:T(256)(128)(2,1)S(1)}, bf16[256]{0:T(256)(128)(2,1)S(1)}, u32[]{:S(2)}, u32[]{:S(2)}) collective-permute-start(bf16[256]{0:T(256)(128)(2,1)S(1)} %collective-permute-done.4), channel_id=1, source_target_pairs={{0,1},{1,2},{2,3},{3,4},{4,5},{5,6},{6,7},{7,0},{8,9},{9,10},{10,1... | collective-permute-start | bytes 1544 | tf_op jit(solution)/shard_map/ppermute | solution.py:16
  118.1 157.9 %reduce-scatter.2.cloned.1.call-start = ((), (), s32[]{:S(2)}) async-start(), calls=%async_computation.6 | async-start | bytes 10616832 | tf_op jit(solution)/shard_map/reduce_scatter | solution.py:110
  172.1 3.7 %copy-start.2 = (bf16[1,2,1024,720]{2,3,1,0:T(8,128)(2,1)S(1)}, bf16[1,2,1024,720]{2,3,1,0:T(8,128)(2,1)}, u32[]{:S(2)}) copy-start(bf16[1,2,1024,720]{2,3,1,0:T(8,128)(2,1)} %param.17) | copy-start | bytes 8847364
  199.9 109.3 %copy-start.1 = (f32[96,2]{0,1:T(2,128)S(1)}, f32[96,2]{0,1:T(2,128)}, u32[]{:S(2)}) copy-start(f32[96,2]{0,1:T(2,128)} %param.11) | copy-start | bytes 2308
  275.9 33.2 %all-to-all-start.2 = ((bf16[4,64,2304]{2,1,0:T(8,128)(2,1)}), bf16[4,64,2304]{2,1,0:T(8,128)(2,1)}, u32[]{:S(2)}, u32[]{:S(2)}) async-start(bf16[4,64,2304]{2,1,0:T(8,128)(2,1)} %bitcast.62), calls=%async_computation.3 | async-start | bytes 2359296 | tf_op jit(solution)/shard_map/all_to_all | solution.py:119
Sparse Core Ops, SparseCore 0:
  52.8 57.9 all-gather.1
  118.2 52.9 all-reduce.2
  200.1 75.8 reduce-scatter.1
